TPU v7x, 32 devices: a whole 2x2x4 slice. The times are simulated.
32 devices in a mesh: groups: 2 (over x), tile: 16 (over z, y, core).
Axes of the slice: x: 2, y: 2, z: 4, core: 2. Of those that a mesh axis runs over, the one named last changes fastest.
Arguments:
- exposures: float32 [32, 8, 256, 256], P(('groups', 'tile')), parts along dimension 0, may hold values from -2400 to 2400
- row_taps: bfloat16 [5, 21], replicated, may hold values from -1.25 to 1.25
- col_taps: bfloat16 [5, 21], replicated, may hold values from -1.25 to 1.25
- kernel_coeffs: float32 [32, 8, 25, 6], P(('groups', 'tile')), parts along dimension 0, may hold values from -1.25 to 1.25
- subpixel: float32 [32, 8, 2], P(('groups', 'tile')), parts along dimension 0, may hold values from 0.1 to 0.9
- destination: int32 [32, 32], P('groups'), parts along dimension 0, may hold values from 0 to 63, as said below
Outputs:
- significance: float32 [32, 8, 4, 128, 128], P(('groups', 'tile')), parts along dimension 0
There are 2 independent parts, one for each index of `groups`. A program takes and returns all parts, laid end to end along the dimension named above; an argument that names none is the same for every part. Nothing has to cross between parts.
Inputs may be any that keep to these rules, and one draw needn't show every extreme that they name: `destination`: entry [t, v * 4 + i] is the sky slot of block i of visit v of tile t; the slots o * 4 to (o + 1) * 4 - 1 are the patches of tile index o. Of the blocks of the 1 tiles of one tile index, at most 2 name slots of one tile index, and in every draw some tile index receives exactly 2 blocks from every tile index.
All inputs are finite; a program needn't handle non-finite values.
Results may differ from a plain program's by a relative error of at most 0.0062.
Values sent between devices are 32-bit elements; how exact they have to be, the bound alone decides.
No kernel may reach another device: no remote copies, remote signals or barrier semaphores. Data moves between devices by JAX's collectives and lax.ppermute only.
A program may use at most 128 MiB of HBM per device.

v0:
```python
import jax
import jax.numpy as jnp
from jax import lax
from jax.sharding import PartitionSpec as P

BLOCK = 128
highest = lax.Precision.HIGHEST


def banded(filter_taps, length):
    tap_count = filter_taps.shape[1]
    middle = tap_count // 2
    pixels = jnp.arange(length, dtype=jnp.int32)
    offset = pixels[None, :] - pixels[:, None] + middle
    selector = (offset[:, :, None] == jnp.arange(tap_count, dtype=jnp.int32)[None, None, :]).astype(
        jnp.bfloat16
    )
    matrix = jnp.einsum("pqk,fk->fpq", selector, filter_taps, preferred_element_type=jnp.float32)
    return matrix.astype(jnp.bfloat16)


def monomials(length):
    coordinate = 2.0 * jnp.arange(length, dtype=jnp.float32) / (length - 1) - 1.0
    unity = jnp.ones((length, length), jnp.float32)
    along_rows = coordinate[:, None] * unity
    along_cols = coordinate[None, :] * unity
    return jnp.stack(
        [
            unity,
            along_rows,
            along_cols,
            along_rows * along_rows,
            along_rows * along_cols,
            along_cols * along_cols,
        ]
    )


def match_one(picture, coeffs, row_stack, col_stack, mono_maps):
    length = picture.shape[0]
    filters = col_stack.shape[0] // length
    smooth = jnp.dot(
        picture.astype(jnp.bfloat16), row_stack, preferred_element_type=jnp.float32
    ).astype(jnp.bfloat16)
    basis_maps = jnp.dot(col_stack, smooth, preferred_element_type=jnp.float32)
    basis_maps = basis_maps.reshape(filters, length, filters, length)
    poly_maps = jnp.einsum(
        "aybx,abj->jyx", basis_maps, coeffs.reshape(filters, filters, -1), precision=highest
    )
    return jnp.sum(mono_maps * poly_maps, axis=0)


def lanczos_matrix(offset_px, block_side):
    pixels = jnp.arange(block_side, dtype=jnp.float32)
    distance = pixels[:, None] - pixels[None, :] + offset_px[..., None, None]
    kernel = jnp.sinc(distance) * jnp.sinc(distance / 3.0)
    return jnp.where(jnp.abs(distance) < 3.0, kernel, 0.0)


def warp_blocks(blocks, shifts):
    block_side = blocks.shape[-1]
    vertical = lanczos_matrix(shifts[..., 0], block_side)
    horizontal = lanczos_matrix(shifts[..., 1], block_side)
    partial_value = jnp.einsum("...ji,...ik->...jk", vertical, blocks, precision=highest)
    return jnp.einsum("...jk,...lk->...jl", partial_value, horizontal, precision=highest)


def lookup(table, index):
    visit_hits = (index[..., None] == jnp.arange(table.shape[0], dtype=jnp.int32)).astype(
        table.dtype
    )
    return jnp.sum(visit_hits * table, axis=-1)


def assemble(contrib, in_slot, in_weight, owned):
    select = (jnp.arange(owned, dtype=jnp.int32)[:, None] == in_slot[None, :]).astype(
        jnp.float32
    ) * in_weight[None, :]
    numerator = jnp.dot(select, contrib, precision=highest, preferred_element_type=jnp.float32)
    denominator = jnp.sum(select, axis=1)
    return numerator / jnp.where(denominator > 0, denominator, 1.0)[:, None]


def per_device(exposures, row_taps, col_taps, kernel_coeffs, subpixel, destination):
    tile_count, visits, length = (exposures.shape[0], exposures.shape[1], exposures.shape[2])
    filters = row_taps.shape[0]
    devices = lax.axis_size("tile")
    own_index = lax.axis_index("tile")
    block_side = BLOCK
    per_side = length // block_side
    block_count = per_side * per_side
    owned = tile_count * block_count
    per_dev = tile_count * visits * block_count
    capacity = 2 * tile_count
    row_stack = jnp.transpose(banded(row_taps, length), (2, 0, 1)).reshape(length, filters * length)
    col_stack = banded(col_taps, length).reshape(filters * length, length)
    mono_maps = monomials(length)
    images = exposures.reshape(tile_count * visits, length, length)
    coeffs = kernel_coeffs.reshape(tile_count * visits, filters * filters, -1)
    matched = lax.map(
        lambda packed: match_one(packed[0], packed[1], row_stack, col_stack, mono_maps),
        (images, coeffs),
    )
    power_sum = jnp.sum((matched * matched).reshape(tile_count, visits, -1), axis=(0, 2))
    power_all = lax.psum(power_sum, "tile")
    variance = power_all / (tile_count * devices * length * length) + 1e-05
    blocks = matched.reshape(tile_count * visits, per_side, block_side, per_side, block_side)
    blocks = blocks.transpose(0, 1, 3, 2, 4).reshape(per_dev, block_side, block_side)
    shifts = jnp.repeat(subpixel.reshape(tile_count * visits, 2), block_count, axis=0)
    local_dest = lax.dynamic_slice_in_dim(
        destination, own_index * tile_count, tile_count, 0
    ).reshape(per_dev)
    local_visit = jnp.arange(per_dev, dtype=jnp.int32) // block_count % visits
    local_scale = jnp.sqrt(lookup(variance, local_visit))
    local_owner = local_dest // owned
    owner_hits = (local_owner[:, None] == jnp.arange(devices, dtype=jnp.int32)[None, :]).astype(
        jnp.int32
    )
    block_rank = jnp.sum((jnp.cumsum(owner_hits, axis=0) - 1) * owner_hits, axis=1)
    position = local_owner * capacity + block_rank
    send_order = (
        jnp.full((devices * capacity,), per_dev, jnp.int32)
        .at[position]
        .set(jnp.arange(per_dev, dtype=jnp.int32))
    )
    is_mine = (destination // owned == own_index).astype(jnp.int32)
    arrival = jnp.cumsum(is_mine, axis=1) - 1
    chosen = is_mine[:, None, :] * (
        arrival[:, None, :] == jnp.arange(capacity, dtype=jnp.int32)[None, :, None]
    ).astype(jnp.int32)
    filled = jnp.sum(chosen, axis=2).reshape(-1)
    in_slot = jnp.sum(chosen * (destination % owned)[:, None, :], axis=2).reshape(-1)
    in_visit = jnp.sum(chosen * local_visit[None, None, :], axis=2).reshape(-1)
    in_weight = filled.astype(jnp.float32) / lookup(variance, in_visit)
    warped_own = warp_blocks(blocks, shifts)
    padded = jnp.concatenate(
        [warped_own, jnp.zeros((1, block_side, block_side), jnp.float32)], axis=0
    )
    outgoing = jnp.take(padded, send_order, axis=0).reshape(
        devices, capacity, block_side, block_side
    )
    arrived = lax.all_to_all(outgoing, "tile", split_axis=0, concat_axis=0, tiled=True)
    template = assemble(
        arrived.reshape(devices * capacity, block_side * block_side), in_slot, in_weight, owned
    )
    at_slots = jnp.take(template, in_slot, axis=0).reshape(
        devices, capacity, block_side, block_side
    )
    returned = lax.all_to_all(at_slots, "tile", split_axis=0, concat_axis=0, tiled=True)
    mine_back = jnp.take(
        returned.reshape(devices * capacity, block_side, block_side), position, axis=0
    )
    result = (warped_own - mine_back) / local_scale[:, None, None]
    return result.reshape(tile_count, visits, block_count, block_side, block_side)


def solution(mesh):
    return jax.shard_map(
        per_device,
        mesh=mesh,
        in_specs=(
            P(("groups", "tile"), None, None, None),
            P(),
            P(),
            P(("groups", "tile"), None, None, None),
            P(("groups", "tile"), None, None),
            P("groups", None),
        ),
        out_specs=P(("groups", "tile"), None, None, None, None),
        check_vma=False,
    )
```

profile of v0, /device:TPU:13, one launch (start us, length us, event | category | flops | bytes accessed | tf_op | source)
XLA Modules:
  0.0 478.9 jit_solution(7830950791814079655)
XLA Ops:
  19.8 290.9 %while.10 = (s32[]{:T(128)}, f32[8,256,256]{2,1,0:T(8,128)}, f32[8,25,6]{1,2,0:T(8,128)S(1)}, bf16[8,256,256]{2,1,0:T(8,128)(2,1)}, bf16[256,1280]{1,0:T(8,128)(...) while((s32[]{:T(128)}, f32[8,256,256]{2,1,0:T(8,128)}, ...), condition=%wide.region_2.4_spmd, body=%wide.region_0.3_spmd.sunk | while | flops 1125646336 | bytes 43125792 | solution.py:100
  24.7 9.1 %reshape.421 = f32[5,256,5,256]{1,0,3,2:T(8,128)} reshape(f32[1280,1280]{0,1:T(8,128)} %convolution_bitcast_fusion.2) | data formatting | bytes 13107200 | tf_op jit(solution)/shard_map/while/body/eval_jaxpr/reshape | solution.py:46
  33.9 9.3 %copy.54 = f32[5,256,5,256]{3,2,0,1:T(8,128)} copy(f32[5,256,5,256]{1,0,3,2:T(8,128)} %reshape.421) | data formatting | bytes 13107200 | tf_op jit(solution)/shard_map/while/body/eval_jaxpr/reshape | solution.py:46
  43.2 12.2 %fusion.248 = f32[256,256]{1,0:T(8,128)S(1)} fusion(f32[6,256,256]{2,0,1:T(8,128)S(1)} %get-tuple-element.153, f32[5,256,5,256]{3,2,0,1:T(8,128)} %copy.54, f32[5,5,6]{1,0,2:T(8,128)S(1)} %reshape.422), kind=kOutput, calls=%fused_computation.7.clone.1 | convolution fusion | flops 118685696 | bytes 8389208 | tf_op jit(solution)/shard_map/while/body/eval_jaxpr/aybx,abj->jyx/dot_general | solution.py:47
  61.1 9.1 %reshape.421 = f32[5,256,5,256]{1,0,3,2:T(8,128)} reshape(f32[1280,1280]{0,1:T(8,128)} %convolution_bitcast_fusion.2) | data formatting | bytes 13107200 | tf_op jit(solution)/shard_map/while/body/eval_jaxpr/reshape | solution.py:46
  70.2 9.3 %copy.54 = f32[5,256,5,256]{3,2,0,1:T(8,128)} copy(f32[5,256,5,256]{1,0,3,2:T(8,128)} %reshape.421) | data formatting | bytes 13107200 | tf_op jit(solution)/shard_map/while/body/eval_jaxpr/reshape | solution.py:46
  79.6 12.2 %fusion.248 = f32[256,256]{1,0:T(8,128)S(1)} fusion(f32[6,256,256]{2,0,1:T(8,128)S(1)} %get-tuple-element.153, f32[5,256,5,256]{3,2,0,1:T(8,128)} %copy.54, f32[5,5,6]{1,0,2:T(8,128)S(1)} %reshape.422), kind=kOutput, calls=%fused_computation.7.clone.1 | convolution fusion | flops 118685696 | bytes 8389208 | tf_op jit(solution)/shard_map/while/body/eval_jaxpr/aybx,abj->jyx/dot_general | solution.py:47
  97.4 9.1 %reshape.421 = f32[5,256,5,256]{1,0,3,2:T(8,128)} reshape(f32[1280,1280]{0,1:T(8,128)} %convolution_bitcast_fusion.2) | data formatting | bytes 13107200 | tf_op jit(solution)/shard_map/while/body/eval_jaxpr/reshape | solution.py:46
  106.6 9.3 %copy.54 = f32[5,256,5,256]{3,2,0,1:T(8,128)} copy(f32[5,256,5,256]{1,0,3,2:T(8,128)} %reshape.421) | data formatting | bytes 13107200 | tf_op jit(solution)/shard_map/while/body/eval_jaxpr/reshape | solution.py:46
  115.9 12.2 %fusion.248 = f32[256,256]{1,0:T(8,128)S(1)} fusion(f32[6,256,256]{2,0,1:T(8,128)S(1)} %get-tuple-element.153, f32[5,256,5,256]{3,2,0,1:T(8,128)} %copy.54, f32[5,5,6]{1,0,2:T(8,128)S(1)} %reshape.422), kind=kOutput, calls=%fused_computation.7.clone.1 | convolution fusion | flops 118685696 | bytes 8389208 | tf_op jit(solution)/shard_map/while/body/eval_jaxpr/aybx,abj->jyx/dot_general | solution.py:47
  142.9 9.3 %copy.54 = f32[5,256,5,256]{3,2,0,1:T(8,128)} copy(f32[5,256,5,256]{1,0,3,2:T(8,128)} %reshape.421) | data formatting | bytes 13107200 | tf_op jit(solution)/shard_map/while/body/eval_jaxpr/reshape | solution.py:46
  152.3 12.2 %fusion.248 = f32[256,256]{1,0:T(8,128)S(1)} fusion(f32[6,256,256]{2,0,1:T(8,128)S(1)} %get-tuple-element.153, f32[5,256,5,256]{3,2,0,1:T(8,128)} %copy.54, f32[5,5,6]{1,0,2:T(8,128)S(1)} %reshape.422), kind=kOutput, calls=%fused_computation.7.clone.1 | convolution fusion | flops 118685696 | bytes 8389208 | tf_op jit(solution)/shard_map/while/body/eval_jaxpr/aybx,abj->jyx/dot_general | solution.py:47
  179.3 9.3 %copy.54 = f32[5,256,5,256]{3,2,0,1:T(8,128)} copy(f32[5,256,5,256]{1,0,3,2:T(8,128)} %reshape.421) | data formatting | bytes 13107200 | tf_op jit(solution)/shard_map/while/body/eval_jaxpr/reshape | solution.py:46
  188.6 12.2 %fusion.248 = f32[256,256]{1,0:T(8,128)S(1)} fusion(f32[6,256,256]{2,0,1:T(8,128)S(1)} %get-tuple-element.153, f32[5,256,5,256]{3,2,0,1:T(8,128)} %copy.54, f32[5,5,6]{1,0,2:T(8,128)S(1)} %reshape.422), kind=kOutput, calls=%fused_computation.7.clone.1 | convolution fusion | flops 118685696 | bytes 8389208 | tf_op jit(solution)/shard_map/while/body/eval_jaxpr/aybx,abj->jyx/dot_general | solution.py:47
  215.6 9.3 %copy.54 = f32[5,256,5,256]{3,2,0,1:T(8,128)} copy(f32[5,256,5,256]{1,0,3,2:T(8,128)} %reshape.421) | data formatting | bytes 13107200 | tf_op jit(solution)/shard_map/while/body/eval_jaxpr/reshape | solution.py:46
  225.0 12.2 %fusion.248 = f32[256,256]{1,0:T(8,128)S(1)} fusion(f32[6,256,256]{2,0,1:T(8,128)S(1)} %get-tuple-element.153, f32[5,256,5,256]{3,2,0,1:T(8,128)} %copy.54, f32[5,5,6]{1,0,2:T(8,128)S(1)} %reshape.422), kind=kOutput, calls=%fused_computation.7.clone.1 | convolution fusion | flops 118685696 | bytes 8389208 | tf_op jit(solution)/shard_map/while/body/eval_jaxpr/aybx,abj->jyx/dot_general | solution.py:47
  252.0 9.3 %copy.54 = f32[5,256,5,256]{3,2,0,1:T(8,128)} copy(f32[5,256,5,256]{1,0,3,2:T(8,128)} %reshape.421) | data formatting | bytes 13107200 | tf_op jit(solution)/shard_map/while/body/eval_jaxpr/reshape | solution.py:46
  261.3 12.2 %fusion.248 = f32[256,256]{1,0:T(8,128)S(1)} fusion(f32[6,256,256]{2,0,1:T(8,128)S(1)} %get-tuple-element.153, f32[5,256,5,256]{3,2,0,1:T(8,128)} %copy.54, f32[5,5,6]{1,0,2:T(8,128)S(1)} %reshape.422), kind=kOutput, calls=%fused_computation.7.clone.1 | convolution fusion | flops 118685696 | bytes 8389208 | tf_op jit(solution)/shard_map/while/body/eval_jaxpr/aybx,abj->jyx/dot_general | solution.py:47
  288.4 9.3 %copy.54 = f32[5,256,5,256]{3,2,0,1:T(8,128)} copy(f32[5,256,5,256]{1,0,3,2:T(8,128)} %reshape.421) | data formatting | bytes 13107200 | tf_op jit(solution)/shard_map/while/body/eval_jaxpr/reshape | solution.py:46
  297.7 12.2 %fusion.248 = f32[256,256]{1,0:T(8,128)S(1)} fusion(f32[6,256,256]{2,0,1:T(8,128)S(1)} %get-tuple-element.153, f32[5,256,5,256]{3,2,0,1:T(8,128)} %copy.54, f32[5,5,6]{1,0,2:T(8,128)S(1)} %reshape.422), kind=kOutput, calls=%fused_computation.7.clone.1 | convolution fusion | flops 118685696 | bytes 8389208 | tf_op jit(solution)/shard_map/while/body/eval_jaxpr/aybx,abj->jyx/dot_general | solution.py:47
  314.8 9.1 %fusion.42 = f32[32,128,128]{2,1,0:T(8,128)S(1)} fusion(f32[32,128,128]{2,1,0:T(8,128)} %bitcast.114, f32[32]{0:T(128)S(1)} %get-tuple-element.85, f32[128,128]{1,0:T(8,128)S(1)} %iota_subtract_fusion), kind=kOutput, calls=%fused_computation.71 | convolution fusion | flops 842530816 | bytes 4259968 | tf_op jit(solution)/shard_map/...ji,...ik->...jk/dot_general | solution.py:64
  324.0 9.2 %fusion.51 = f32[32,128,128]{2,1,0:T(8,128)S(1)} fusion(f32[32,128,128]{2,1,0:T(8,128)S(1)} %fusion.42, f32[32]{0:T(128)S(1)} %get-tuple-element.84, f32[128,128]{1,0:T(8,128)S(1)} %iota_subtract_fusion), kind=kOutput, calls=%fused_computation.78 | convolution fusion | flops 842530816 | bytes 4259968 | tf_op jit(solution)/shard_map/...jk,...lk->...jl/dot_general | solution.py:65
  348.3 62.1 %psum.7 = f32[8]{0:T(128)S(1)} all-reduce(f32[8]{0:T(128)S(1)} %multiply_reduce_fusion), channel_id=1, replica_groups=mesh['groups'=2,'tile'=16] {'tile'}, use_global_device_ids=true, to_apply=%region_10.12 | all-reduce | flops 8 | bytes 64 | tf_op jit(solution)/shard_map/psum | solution.py:105
  423.2 47.4 %all-to-all-done.1 = f32[16,2,128,128]{3,2,1,0:T(8,128)S(1)} async-done(((f32[16,2,128,128]{3,2,1,0:T(8,128)}), f32[16,2,128,128]{3,2,1,0:T(8,128)S(1)}, u32[]{:S(2)}, u32[]{:S(2)}) %all-to-all-start.1) | async-done | bytes 2097184 | tf_op jit(solution)/shard_map/all_to_all | solution.py:149
  (126 shorter events, 151.6 us)
Async XLA Ops:
  0.0 6.0 %copy-start = (bf16[5,21]{1,0:T(8,128)(2,1)S(1)}, bf16[5,21]{1,0:T(8,128)(2,1)}, u32[]{:S(2)}) copy-start(bf16[5,21]{1,0:T(8,128)(2,1)} %param.10) | copy-start | bytes 634
  6.0 1.8 copy-start.7
  312.9 1.6 copy-start.6
  333.2 1.4 copy-start.2
  339.9 71.9 %all-to-all-start = ((f32[16,2,128,128]{3,2,1,0:T(8,128)}), f32[16,2,128,128]{3,2,1,0:T(8,128)S(1)}, u32[]{:S(2)}, u32[]{:S(2)}) async-start(f32[16,2,128,128]{3,2,1,0:T(8,128)} %broadcast_select_fusion.1), calls=%async_computation | async-start | bytes 4194304 | tf_op jit(solution)/shard_map/all_to_all | solution.py:142
  346.4 64.0 %copy-start.5 = (s32[16,32]{1,0:T(8,128)S(1)}, s32[16,32]{1,0:T(8,128)}, u32[]{:S(2)}) copy-start(s32[16,32]{1,0:T(8,128)} %param.14) | copy-start | bytes 6148
  417.2 53.3 %all-to-all-start.1 = ((f32[16,2,128,128]{3,2,1,0:T(8,128)}), f32[16,2,128,128]{3,2,1,0:T(8,128)S(1)}, u32[]{:S(2)}, u32[]{:S(2)}) async-start(f32[16,2,128,128]{3,2,1,0:T(8,128)} %broadcast_select_fusion), calls=%async_computation.1 | async-start | bytes 4194304 | tf_op jit(solution)/shard_map/all_to_all | solution.py:149
  470.6 1.3 copy-start.4
  471.9 3.7 copy-start.3
  471.9 7.0 %copy-start.1 = (bf16[5,21]{1,0:T(8,128)(2,1)S(1)}, bf16[5,21]{1,0:T(8,128)(2,1)}, u32[]{:S(2)}) copy-start(bf16[5,21]{1,0:T(8,128)(2,1)} %param.10) | copy-start | bytes 634
where the time goes:
time: 482 us; the launch traced here: 479 us
  local copies, waits for them, and re-layouts  180 us (37%)
  matrix products  160 us (33%)
  blocking collectives  62.1 us (13%)
  waiting for transfers between devices  47.4 us (10%)
  other arithmetic  16 us (3%)
  starting transfers between devices  12.5 us (3%)
    reshape x16, local copies, waits for them, and re-layouts, match_one(): basis_maps = basis_maps.reshape(filters, length, filters, length)  147 us
    dot_general x8, matrix products, match_one(): jnp.einsum('aybx,abj->jyx', basis_maps, coeffs.reshape(filters, filters,...  97.6 us
    psum x1, blocking collectives, per_device(): power_all = lax.psum(power_sum, 'tile')  62.1 us
    all_to_all x1, waiting for transfers between devices, per_device(): lax.all_to_all(at_slots, 'tile', split_axis=0, concat_axis=0, tiled=True)  47.4 us
    dot_general x8, matrix products, match_one(): basis_maps = jnp.dot(col_stack, smooth, preferred_element_type=jnp.float32)  39.6 us
  transfers between devices with their start and end apart: 2, of which 1 were waited for; matrix products, arithmetic and copies ran while one was open for 1% of the time, Pallas kernels for 0%

commit v1 on v0

--- a/solution.py
+++ b/solution.py
@@ -102,7 +102,10 @@
         (images, coeffs),
     )
     power_sum = jnp.sum((matched * matched).reshape(tile_count, visits, -1), axis=(0, 2))
-    power_all = lax.psum(power_sum, "tile")
+    size, power_all = (lax.axis_size("tile"), power_sum)
+    for far in [1 << k for k in range(size.bit_length() - 1)]:
+        swap = [(i, i ^ far) for i in range(size)]
+        power_all = power_all + lax.ppermute(power_all, "tile", swap)
     variance = power_all / (tile_count * devices * length * length) + 1e-05
     blocks = matched.reshape(tile_count * visits, per_side, block_side, per_side, block_side)
     blocks = blocks.transpose(0, 1, 3, 2, 4).reshape(per_dev, block_side, block_side)

time: 482 us -> 463 us (0.961)
  blocking collectives: 62.1 us -> 0 us
  waiting for transfers between devices: 47.4 us -> 89.5 us
    psum x1 -> x0, blocking collectives: 62.1 us -> none  [per_device(): power_all = lax.psum(power_sum, 'tile')]
    ppermute x0 -> x4, waiting for transfers between devices: none -> 40.1 us  [per_device(): power_all = power_all + lax.ppermute(power_all, 'tile', swap)]
  transfers between devices with their start and end apart: 2 -> 6, of which waited for: 1 -> 5; matrix products, arithmetic and copies ran while one was open for 1% -> 1% of each run, Pallas kernels for 0% -> 0%
where the time goes in v1:
time: 463 us; the launch traced here: 460 us
  local copies, waits for them, and re-layouts  180 us (39%)
  matrix products  161 us (35%)
  waiting for transfers between devices  89.5 us (19%)
  other arithmetic  15 us (3%)
  starting transfers between devices  14.1 us (3%)
    reshape x16, local copies, waits for them, and re-layouts, match_one(): basis_maps = basis_maps.reshape(filters, length, filters, length)  147 us
    dot_general x8, matrix products, match_one(): jnp.einsum('aybx,abj->jyx', basis_maps, coeffs.reshape(filters, filters,...  97.6 us
    all_to_all x1, waiting for transfers between devices, per_device(): lax.all_to_all(at_slots, 'tile', split_axis=0, concat_axis=0, tiled=True)  47.4 us
    ppermute x4, waiting for transfers between devices, per_device(): power_all = power_all + lax.ppermute(power_all, 'tile', swap)  40.1 us
    dot_general x8, matrix products, match_one(): basis_maps = jnp.dot(col_stack, smooth, preferred_element_type=jnp.float32)  39.6 us
    another operation x6, local copies, waits for them, and re-layouts, monomials(): jnp.stack([unity, along_rows, along_cols, along_rows * along_rows, along_...  9.49 us
  transfers between devices with their start and end apart: 6, of which 5 were waited for; matrix products, arithmetic and copies ran while one was open for 1% of the time, Pallas kernels for 0%

profile of v1, /device:TPU:13, one launch (start us, length us, event | category | flops | bytes accessed | tf_op | source)
XLA Modules:
  0.0 460.0 jit_solution(11003813833639923636)
XLA Ops:
  19.2 290.9 %while.10 = (s32[]{:T(128)}, f32[8,256,256]{2,1,0:T(8,128)}, f32[8,25,6]{1,2,0:T(8,128)S(1)}, bf16[8,256,256]{2,1,0:T(8,128)(2,1)}, bf16[256,1280]{1,0:T(8,128)(...) while((s32[]{:T(128)}, f32[8,256,256]{2,1,0:T(8,128)}, ...), condition=%wide.region_2.4_spmd, body=%wide.region_0.3_spmd.sunk | while | flops 1125646336 | bytes 43126800 | solution.py:100
  24.1 9.1 %reshape.421 = f32[5,256,5,256]{1,0,3,2:T(8,128)} reshape(f32[1280,1280]{0,1:T(8,128)} %convolution_bitcast_fusion.2) | data formatting | bytes 13107200 | tf_op jit(solution)/shard_map/while/body/eval_jaxpr/reshape | solution.py:46
  33.3 9.3 %copy.54 = f32[5,256,5,256]{3,2,0,1:T(8,128)} copy(f32[5,256,5,256]{1,0,3,2:T(8,128)} %reshape.421) | data formatting | bytes 13107200 | tf_op jit(solution)/shard_map/while/body/eval_jaxpr/reshape | solution.py:46
  42.6 12.2 %fusion.248 = f32[256,256]{1,0:T(8,128)S(1)} fusion(f32[6,256,256]{2,0,1:T(8,128)S(1)} %get-tuple-element.153, f32[5,256,5,256]{3,2,0,1:T(8,128)} %copy.54, f32[5,5,6]{1,0,2:T(8,128)S(1)} %reshape.422), kind=kOutput, calls=%fused_computation.7.clone.1 | convolution fusion | flops 118685696 | bytes 8389208 | tf_op jit(solution)/shard_map/while/body/eval_jaxpr/aybx,abj->jyx/dot_general | solution.py:47
  60.5 9.1 %reshape.421 = f32[5,256,5,256]{1,0,3,2:T(8,128)} reshape(f32[1280,1280]{0,1:T(8,128)} %convolution_bitcast_fusion.2) | data formatting | bytes 13107200 | tf_op jit(solution)/shard_map/while/body/eval_jaxpr/reshape | solution.py:46
  69.6 9.3 %copy.54 = f32[5,256,5,256]{3,2,0,1:T(8,128)} copy(f32[5,256,5,256]{1,0,3,2:T(8,128)} %reshape.421) | data formatting | bytes 13107200 | tf_op jit(solution)/shard_map/while/body/eval_jaxpr/reshape | solution.py:46
  79.0 12.2 %fusion.248 = f32[256,256]{1,0:T(8,128)S(1)} fusion(f32[6,256,256]{2,0,1:T(8,128)S(1)} %get-tuple-element.153, f32[5,256,5,256]{3,2,0,1:T(8,128)} %copy.54, f32[5,5,6]{1,0,2:T(8,128)S(1)} %reshape.422), kind=kOutput, calls=%fused_computation.7.clone.1 | convolution fusion | flops 118685696 | bytes 8389208 | tf_op jit(solution)/shard_map/while/body/eval_jaxpr/aybx,abj->jyx/dot_general | solution.py:47
  96.8 9.1 %reshape.421 = f32[5,256,5,256]{1,0,3,2:T(8,128)} reshape(f32[1280,1280]{0,1:T(8,128)} %convolution_bitcast_fusion.2) | data formatting | bytes 13107200 | tf_op jit(solution)/shard_map/while/body/eval_jaxpr/reshape | solution.py:46
  106.0 9.3 %copy.54 = f32[5,256,5,256]{3,2,0,1:T(8,128)} copy(f32[5,256,5,256]{1,0,3,2:T(8,128)} %reshape.421) | data formatting | bytes 13107200 | tf_op jit(solution)/shard_map/while/body/eval_jaxpr/reshape | solution.py:46
  115.3 12.2 %fusion.248 = f32[256,256]{1,0:T(8,128)S(1)} fusion(f32[6,256,256]{2,0,1:T(8,128)S(1)} %get-tuple-element.153, f32[5,256,5,256]{3,2,0,1:T(8,128)} %copy.54, f32[5,5,6]{1,0,2:T(8,128)S(1)} %reshape.422), kind=kOutput, calls=%fused_computation.7.clone.1 | convolution fusion | flops 118685696 | bytes 8389208 | tf_op jit(solution)/shard_map/while/body/eval_jaxpr/aybx,abj->jyx/dot_general | solution.py:47
  142.3 9.3 %copy.54 = f32[5,256,5,256]{3,2,0,1:T(8,128)} copy(f32[5,256,5,256]{1,0,3,2:T(8,128)} %reshape.421) | data formatting | bytes 13107200 | tf_op jit(solution)/shard_map/while/body/eval_jaxpr/reshape | solution.py:46
  151.7 12.2 %fusion.248 = f32[256,256]{1,0:T(8,128)S(1)} fusion(f32[6,256,256]{2,0,1:T(8,128)S(1)} %get-tuple-element.153, f32[5,256,5,256]{3,2,0,1:T(8,128)} %copy.54, f32[5,5,6]{1,0,2:T(8,128)S(1)} %reshape.422), kind=kOutput, calls=%fused_computation.7.clone.1 | convolution fusion | flops 118685696 | bytes 8389208 | tf_op jit(solution)/shard_map/while/body/eval_jaxpr/aybx,abj->jyx/dot_general | solution.py:47
  178.7 9.3 %copy.54 = f32[5,256,5,256]{3,2,0,1:T(8,128)} copy(f32[5,256,5,256]{1,0,3,2:T(8,128)} %reshape.421) | data formatting | bytes 13107200 | tf_op jit(solution)/shard_map/while/body/eval_jaxpr/reshape | solution.py:46
  188.0 12.2 %fusion.248 = f32[256,256]{1,0:T(8,128)S(1)} fusion(f32[6,256,256]{2,0,1:T(8,128)S(1)} %get-tuple-element.153, f32[5,256,5,256]{3,2,0,1:T(8,128)} %copy.54, f32[5,5,6]{1,0,2:T(8,128)S(1)} %reshape.422), kind=kOutput, calls=%fused_computation.7.clone.1 | convolution fusion | flops 118685696 | bytes 8389208 | tf_op jit(solution)/shard_map/while/body/eval_jaxpr/aybx,abj->jyx/dot_general | solution.py:47
  215.0 9.3 %copy.54 = f32[5,256,5,256]{3,2,0,1:T(8,128)} copy(f32[5,256,5,256]{1,0,3,2:T(8,128)} %reshape.421) | data formatting | bytes 13107200 | tf_op jit(solution)/shard_map/while/body/eval_jaxpr/reshape | solution.py:46
  224.4 12.2 %fusion.248 = f32[256,256]{1,0:T(8,128)S(1)} fusion(f32[6,256,256]{2,0,1:T(8,128)S(1)} %get-tuple-element.153, f32[5,256,5,256]{3,2,0,1:T(8,128)} %copy.54, f32[5,5,6]{1,0,2:T(8,128)S(1)} %reshape.422), kind=kOutput, calls=%fused_computation.7.clone.1 | convolution fusion | flops 118685696 | bytes 8389208 | tf_op jit(solution)/shard_map/while/body/eval_jaxpr/aybx,abj->jyx/dot_general | solution.py:47
  251.4 9.3 %copy.54 = f32[5,256,5,256]{3,2,0,1:T(8,128)} copy(f32[5,256,5,256]{1,0,3,2:T(8,128)} %reshape.421) | data formatting | bytes 13107200 | tf_op jit(solution)/shard_map/while/body/eval_jaxpr/reshape | solution.py:46
  260.7 12.2 %fusion.248 = f32[256,256]{1,0:T(8,128)S(1)} fusion(f32[6,256,256]{2,0,1:T(8,128)S(1)} %get-tuple-element.153, f32[5,256,5,256]{3,2,0,1:T(8,128)} %copy.54, f32[5,5,6]{1,0,2:T(8,128)S(1)} %reshape.422), kind=kOutput, calls=%fused_computation.7.clone.1 | convolution fusion | flops 118685696 | bytes 8389208 | tf_op jit(solution)/shard_map/while/body/eval_jaxpr/aybx,abj->jyx/dot_general | solution.py:47
  287.8 9.3 %copy.54 = f32[5,256,5,256]{3,2,0,1:T(8,128)} copy(f32[5,256,5,256]{1,0,3,2:T(8,128)} %reshape.421) | data formatting | bytes 13107200 | tf_op jit(solution)/shard_map/while/body/eval_jaxpr/reshape | solution.py:46
  297.1 12.2 %fusion.248 = f32[256,256]{1,0:T(8,128)S(1)} fusion(f32[6,256,256]{2,0,1:T(8,128)S(1)} %get-tuple-element.153, f32[5,256,5,256]{3,2,0,1:T(8,128)} %copy.54, f32[5,5,6]{1,0,2:T(8,128)S(1)} %reshape.422), kind=kOutput, calls=%fused_computation.7.clone.1 | convolution fusion | flops 118685696 | bytes 8389208 | tf_op jit(solution)/shard_map/while/body/eval_jaxpr/aybx,abj->jyx/dot_general | solution.py:47
  314.2 9.1 %fusion.42 = f32[32,128,128]{2,1,0:T(8,128)S(1)} fusion(f32[32,128,128]{2,1,0:T(8,128)} %bitcast.114, f32[32]{0:T(128)S(1)} %get-tuple-element.85, f32[128,128]{1,0:T(8,128)S(1)} %iota_subtract_fusion), kind=kOutput, calls=%fused_computation.71 | convolution fusion | flops 842530816 | bytes 4259968 | tf_op jit(solution)/shard_map/...ji,...ik->...jk/dot_general | solution.py:64
  323.4 9.2 %fusion.51 = f32[32,128,128]{2,1,0:T(8,128)S(1)} fusion(f32[32,128,128]{2,1,0:T(8,128)S(1)} %fusion.42, f32[32]{0:T(128)S(1)} %get-tuple-element.84, f32[128,128]{1,0:T(8,128)S(1)} %iota_subtract_fusion), kind=kOutput, calls=%fused_computation.78 | convolution fusion | flops 842530816 | bytes 4259968 | tf_op jit(solution)/shard_map/...jk,...lk->...jl/dot_general | solution.py:65
  355.7 25.4 %collective-permute-done.2 = f32[8]{0:T(128)S(1)} collective-permute-done((f32[8]{0:T(128)S(1)}, f32[8]{0:T(128)S(1)}, u32[]{:S(2)}, u32[]{:S(2)}) %collective-permute-start.2) | collective-permute-done | bytes 64 | tf_op jit(solution)/shard_map/ppermute | solution.py:108
  404.3 47.4 %all-to-all-done.1 = f32[16,2,128,128]{3,2,1,0:T(8,128)S(1)} async-done(((f32[16,2,128,128]{3,2,1,0:T(8,128)}), f32[16,2,128,128]{3,2,1,0:T(8,128)S(1)}, u32[]{:S(2)}, u32[]{:S(2)}) %all-to-all-start.1) | async-done | bytes 2097184 | tf_op jit(solution)/shard_map/all_to_all | solution.py:152
  (144 shorter events, 169.3 us)
Async XLA Ops:
  0.0 4.2 copy-start
  0.1 5.6 %copy-start.6 = (s32[256,256]{1,0:T(8,128)}, s32[256,256]{1,0:T(8,128)S(1)}, u32[]{:S(2)}) copy-start(s32[256,256]{1,0:T(8,128)S(1)} %subtract_add_fusion) | copy-start | bytes 786436
  4.2 1.8 copy-start.11
  5.7 2.9 copy-start.5
  8.4 1.3 copy-start.8
  19.2 290.9 %copy-start.10 = (s32[32]{0:T(128)S(1)}, s32[32]{0:T(128)}, u32[]{:S(2)}) copy-start(s32[32]{0:T(128)} %compare_select_fusion.3) | copy-start | bytes 388
  312.3 1.6 copy-start.9
  332.6 1.4 copy-start.2
  339.3 54.0 %all-to-all-start = ((f32[16,2,128,128]{3,2,1,0:T(8,128)}), f32[16,2,128,128]{3,2,1,0:T(8,128)S(1)}, u32[]{:S(2)}, u32[]{:S(2)}) async-start(f32[16,2,128,128]{3,2,1,0:T(8,128)} %broadcast_select_fusion.1), calls=%async_computation | async-start | bytes 4194304 | tf_op jit(solution)/shard_map/all_to_all | solution.py:145
  345.8 2.3 copy-start.7
  347.7 1.6 collective-permute-start
  349.3 6.1 %collective-permute-start.1 = (f32[8]{0:T(128)S(1)}, f32[8]{0:T(128)S(1)}, u32[]{:S(2)}, u32[]{:S(2)}) collective-permute-start(f32[8]{0:T(128)S(1)} %add.239), channel_id=1, source_target_pairs={{0,2},{1,3},{2,0},{3,1},{4,6},{5,7},{6,4},{7,5},{8,10},{9,11},{10,... | collective-permute-start | bytes 104 | tf_op jit(solution)/shard_map/ppermute | solution.py:108
  355.4 25.7 %collective-permute-start.2 = (f32[8]{0:T(128)S(1)}, f32[8]{0:T(128)S(1)}, u32[]{:S(2)}, u32[]{:S(2)}) collective-permute-start(f32[8]{0:T(128)S(1)} %add.240), channel_id=1, source_target_pairs={{0,4},{1,5},{2,6},{3,7},{4,0},{5,1},{6,2},{7,3},{8,12},{9,13},{10,... | collective-permute-start | bytes 104 | tf_op jit(solution)/shard_map/ppermute | solution.py:108
  381.2 9.9 %collective-permute-start.3 = (f32[8]{0:T(128)S(1)}, f32[8]{0:T(128)S(1)}, u32[]{:S(2)}, u32[]{:S(2)}) collective-permute-start(f32[8]{0:T(128)S(1)} %add.241), channel_id=1, source_target_pairs={{0,8},{1,9},{2,10},{3,11},{4,12},{5,13},{6,14},{7,15},{8,0},{9,1},... | collective-permute-start | bytes 104 | tf_op jit(solution)/shard_map/ppermute | solution.py:108
  398.7 53.0 %all-to-all-start.1 = ((f32[16,2,128,128]{3,2,1,0:T(8,128)}), f32[16,2,128,128]{3,2,1,0:T(8,128)S(1)}, u32[]{:S(2)}, u32[]{:S(2)}) async-start(f32[16,2,128,128]{3,2,1,0:T(8,128)} %broadcast_select_fusion), calls=%async_computation.1 | async-start | bytes 4194304 | tf_op jit(solution)/shard_map/all_to_all | solution.py:152
  451.7 1.3 copy-start.4
  453.0 3.7 copy-start.3
  453.0 7.0 %copy-start.1 = (bf16[5,21]{1,0:T(8,128)(2,1)S(1)}, bf16[5,21]{1,0:T(8,128)(2,1)}, u32[]{:S(2)}) copy-start(bf16[5,21]{1,0:T(8,128)(2,1)} %param.10) | copy-start | bytes 634
